TPU v7x, 128 devices: a whole 4x4x4 slice. The times are simulated.
128 devices in a mesh: group: 4 (over y_hi, core), blk: 32 (over y_lo, z, x).
Axes of the slice: x: 4, y: 4 (y_hi: 2, y_lo: 2; y = y_hi * 2 + y_lo), z: 4, core: 2. Of those that a mesh axis runs over, the one named last changes fastest.
Arguments:
- points: bfloat16 [1048576, 768], P(('group', 'blk')), may hold values from -128 to 128
- block_lists: int32 [8192, 4], P(('group', 'blk')), may hold values from 0 to 511, as said below
- centroids: bfloat16 [32768, 768], P('blk'), may hold values from -6 to 6
- dual_weights: bfloat16 [32768], P('blk'), may hold values from -1 to 1
Outputs:
- new_centroids: bfloat16 [32768, 768], P('blk')
- new_weights: bfloat16 [32768], P('blk')
Inputs may be any that keep to these rules, and one draw needn't show every extreme that they name: `block_lists`: cycle position q (index q along blk) owns blocks q * 16 to (q + 1) * 16 - 1. For a tile held by a device at cycle position p, slot 0 names a block of position p - 1, slot 2 a block of position p + 1, and slots 1 and 3 two different blocks of position p, positions taken modulo the number of devices along blk.
All inputs are finite; a program needn't handle non-finite values.
Results may differ from a plain program's by a relative error of at most 0.0052.
Values may be sent and summed in bfloat16 or wider, within the bound.
A program may use at most 128 MiB of HBM per device.

v0:
```python
import math

import jax
import jax.numpy as jnp
from jax import lax
from jax.sharding import PartitionSpec as P

D = 768
BLOCK = 64
TILE = 128
SLOTS = 4
ITERS = 2


prior_mass = 1.0
dual_step = 0.5


def passed_along(block, axis, distance):
    devices = range(lax.axis_size(axis))
    route = [((i - distance) % len(devices), i) for i in devices]
    return lax.ppermute(block, axis, route)


def with_halo(cells, sides, width):
    for axis, dim in sides:
        count = lax.axis_size(axis)
        head = lax.slice_in_dim(cells, 0, width, axis=dim)
        tail = lax.slice_in_dim(cells, cells.shape[dim] - width, cells.shape[dim], axis=dim)
        cells = jnp.concatenate(
            [
                lax.ppermute(tail, axis, [(i, (i + 1) % count) for i in range(count)]),
                cells,
                lax.ppermute(head, axis, [((i + 1) % count, i) for i in range(count)]),
            ],
            axis=dim,
        )
    return cells


def renew_blocks(numerator, masses, centroids, weights, target):
    base = centroids.astype(jnp.float32)
    fresh = ((numerator + prior_mass * base) / (masses + prior_mass)[:, None]).astype(jnp.bfloat16)
    renewed = (weights.astype(jnp.float32) + dual_step * (1.0 - masses / target)).astype(
        jnp.bfloat16
    )
    return (fresh, renewed)


def return_cycle(near_num, near_mass):
    upper_num, upper_mass = passed_along((near_num[0], near_mass[0]), "blk", -1)
    lower_num, lower_mass = passed_along((near_num[2], near_mass[2]), "blk", 1)
    return (near_num[1] + upper_num + lower_num, near_mass[1] + upper_mass + lower_mass)


def assign_tiles(points, near_ids, near_centroids, offsets):
    tile_count = near_ids.shape[0]
    group_size = math.gcd(tile_count, 8)
    block_total = near_centroids.shape[0] // BLOCK
    width = points.shape[1]
    cand_flat = near_centroids.reshape(block_total, BLOCK * width)
    offset_blocks = offsets.reshape(block_total, BLOCK)
    tiled_points = points.reshape(tile_count // group_size, group_size, TILE, width)
    tiled_ids = near_ids.reshape(tile_count // group_size, group_size, SLOTS)
    block_iota = jnp.arange(block_total, dtype=jnp.int32)

    def tile_step(running, packet):
        sum_num, sum_mass = running
        tile_points, block_ids = packet
        picker = block_ids.reshape(-1)[:, None] == block_iota[None, :]
        candidates = jnp.dot(
            picker.astype(jnp.bfloat16), cand_flat, preferred_element_type=jnp.float32
        ).astype(jnp.bfloat16)
        candidates = candidates.reshape(group_size, SLOTS * BLOCK, width)
        picker_f = picker.astype(jnp.float32)
        cand_offsets = jnp.dot(
            picker_f,
            offset_blocks,
            precision=lax.Precision.HIGHEST,
            preferred_element_type=jnp.float32,
        )
        scores = jnp.einsum(
            "tpd,tkd->tpk", tile_points, candidates, preferred_element_type=jnp.float32
        ) * (32.0 / width)
        scores = scores + cand_offsets.reshape(group_size, 1, SLOTS * BLOCK)
        membership = jax.nn.softmax(scores, axis=-1).astype(jnp.bfloat16)
        masses = jnp.sum(membership.astype(jnp.float32), axis=1).reshape(group_size * SLOTS, BLOCK)
        numerator = jnp.einsum(
            "tpk,tpd->tkd", membership, tile_points, preferred_element_type=jnp.float32
        )
        numerator = numerator.reshape(group_size * SLOTS, BLOCK * width)
        add_num = jnp.dot(
            picker_f.T,
            numerator,
            precision=lax.Precision.HIGHEST,
            preferred_element_type=jnp.float32,
        )
        add_mass = jnp.dot(
            picker_f.T, masses, precision=lax.Precision.HIGHEST, preferred_element_type=jnp.float32
        )
        return ((sum_num + add_num, sum_mass + add_mass), None)

    start = (
        jnp.zeros((block_total, BLOCK * width), jnp.float32),
        jnp.zeros((block_total, BLOCK), jnp.float32),
    )
    (sum_num, sum_mass), _ = lax.scan(tile_step, start, (tiled_points, tiled_ids))
    return (sum_num.reshape(3, -1, width), sum_mass.reshape(3, -1))


def per_device(points, block_lists, centroids, dual_weights):
    own_rows = centroids.shape[0]
    own_blocks = own_rows // BLOCK
    cycle_size = lax.axis_size("blk")
    position = lax.axis_index("blk")
    groups = lax.axis_size("group")
    target = points.shape[0] * groups / own_rows
    owner = block_lists // own_blocks
    near_ids = (owner - position + 1) % cycle_size * own_blocks + block_lists % own_blocks
    weights = dual_weights
    for sweep in range(ITERS):
        near_centroids, near_weights = (
            with_halo(centroids, (("blk", 0),), own_rows),
            with_halo(weights, (("blk", 0),), own_rows),
        )
        squares = jnp.sum(jnp.square(near_centroids.astype(jnp.float32)), axis=1)
        offsets = near_weights.astype(jnp.float32) - squares * (16.0 / D)
        near_num, near_mass = assign_tiles(points, near_ids, near_centroids, offsets)
        own_num, own_mass = return_cycle(near_num, near_mass)
        total_num, total_mass = lax.psum((own_num, own_mass), "group")
        centroids, weights = renew_blocks(total_num, total_mass, centroids, weights, target)
    return (centroids, weights)


def solution(mesh):
    return jax.shard_map(
        per_device,
        mesh=mesh,
        in_specs=(P(("group", "blk"), None), P(("group", "blk"), None), P("blk", None), P("blk")),
        out_specs=(P("blk", None), P("blk")),
        check_vma=False,
    )
```

profile of v0, /device:TPU:1, one launch (start us, length us, event | category | flops | bytes accessed | tf_op | source)
XLA Modules:
  0.0 988.7 jit_solution(7902707042533169863)
XLA Ops:
  9.3 5.8 collective-permute-start.1
  15.2 5.7 collective-permute-start.3
  22.4 27.2 %collective-permute-done.2 = bf16[1024]{0:T(1024)(128)(2,1)S(1)} collective-permute-done((bf16[1024]{0:T(1024)(128)(2,1)}, bf16[1024]{0:T(1024)(128)(2,1)S(1)}, u32[]{:S(2)}, u32[]{:S(2)}) %collective-permute-start.2) | collective-permute-done | bytes 2080 | tf_op jit(solution)/shard_map/ppermute | solution.py:32
  55.0 6.9 reshape.98
  65.2 258.4 %while.26 = (s32[]{:T(128)}, f32[48,49152]{1,0:T(8,128)}, f32[48,64]{1,0:T(8,128)S(1)}, s32[8,8,4]{2,1,0:T(8,128)S(1)}, bf16[8,8,128,768]{3,2,1,0:T(8,128)(2,1)}...) while((s32[]{:T(128)}, f32[48,49152]{1,0:T(8,128)}, ...), condition=%wide.region_5.6_spmd.clone, body=%wide.region_1.5_spmd.clone.sunk | while | flops 1873029376 | bytes 67745896 | solution.py:107
  75.8 5.0 fusion.108
  80.8 6.2 reshape.113
  87.1 8.9 convolution_add_fusion.8
  106.9 5.0 fusion.108
  111.9 6.2 reshape.113
  118.1 10.3 %convolution_add_fusion.8 = f32[48,49152]{1,0:T(8,128)} fusion(f32[32,49152]{1,0:T(8,128)} %reshape.113, f32[48,49152]{1,0:T(8,128)} %get-tuple-element.310, pred[]{:T(512)S(6)} %compare.10, s32[32]{0:T(128)S(1)} %eq.109), kind=kOutput, calls=%fused_computation.3.clone.1 | convolution fusion | flops 910689792 | bytes 25165952 | tf_op jit(solution)/shard_map/while/body/eval_jaxpr/dot_general | solution.py:92
  139.3 5.0 fusion.108
  144.4 6.2 reshape.113
  150.6 10.3 %convolution_add_fusion.8 = f32[48,49152]{1,0:T(8,128)} fusion(f32[32,49152]{1,0:T(8,128)} %reshape.113, f32[48,49152]{1,0:T(8,128)} %get-tuple-element.310, pred[]{:T(512)S(6)} %compare.10, s32[32]{0:T(128)S(1)} %eq.109), kind=kOutput, calls=%fused_computation.3.clone.1 | convolution fusion | flops 910689792 | bytes 25165952 | tf_op jit(solution)/shard_map/while/body/eval_jaxpr/dot_general | solution.py:92
  171.8 5.0 fusion.108
  176.9 6.2 reshape.113
  183.1 10.3 %convolution_add_fusion.8 = f32[48,49152]{1,0:T(8,128)} fusion(f32[32,49152]{1,0:T(8,128)} %reshape.113, f32[48,49152]{1,0:T(8,128)} %get-tuple-element.310, pred[]{:T(512)S(6)} %compare.10, s32[32]{0:T(128)S(1)} %eq.109), kind=kOutput, calls=%fused_computation.3.clone.1 | convolution fusion | flops 910689792 | bytes 25165952 | tf_op jit(solution)/shard_map/while/body/eval_jaxpr/dot_general | solution.py:92
  204.3 5.0 fusion.108
  209.4 6.2 reshape.113
  215.6 10.3 %convolution_add_fusion.8 = f32[48,49152]{1,0:T(8,128)} fusion(f32[32,49152]{1,0:T(8,128)} %reshape.113, f32[48,49152]{1,0:T(8,128)} %get-tuple-element.310, pred[]{:T(512)S(6)} %compare.10, s32[32]{0:T(128)S(1)} %eq.109), kind=kOutput, calls=%fused_computation.3.clone.1 | convolution fusion | flops 910689792 | bytes 25165952 | tf_op jit(solution)/shard_map/while/body/eval_jaxpr/dot_general | solution.py:92
  236.8 5.0 fusion.108
  241.8 6.2 reshape.113
  248.0 10.3 %convolution_add_fusion.8 = f32[48,49152]{1,0:T(8,128)} fusion(f32[32,49152]{1,0:T(8,128)} %reshape.113, f32[48,49152]{1,0:T(8,128)} %get-tuple-element.310, pred[]{:T(512)S(6)} %compare.10, s32[32]{0:T(128)S(1)} %eq.109), kind=kOutput, calls=%fused_computation.3.clone.1 | convolution fusion | flops 910689792 | bytes 25165952 | tf_op jit(solution)/shard_map/while/body/eval_jaxpr/dot_general | solution.py:92
  269.3 5.0 fusion.108
  274.3 6.2 reshape.113
  280.5 10.3 %convolution_add_fusion.8 = f32[48,49152]{1,0:T(8,128)} fusion(f32[32,49152]{1,0:T(8,128)} %reshape.113, f32[48,49152]{1,0:T(8,128)} %get-tuple-element.310, pred[]{:T(512)S(6)} %compare.10, s32[32]{0:T(128)S(1)} %eq.109), kind=kOutput, calls=%fused_computation.3.clone.1 | convolution fusion | flops 910689792 | bytes 25165952 | tf_op jit(solution)/shard_map/while/body/eval_jaxpr/dot_general | solution.py:92
  301.7 5.0 fusion.108
  306.8 6.2 reshape.113
  313.0 10.3 %convolution_add_fusion.8 = f32[48,49152]{1,0:T(8,128)} fusion(f32[32,49152]{1,0:T(8,128)} %reshape.113, f32[48,49152]{1,0:T(8,128)} %get-tuple-element.310, pred[]{:T(512)S(6)} %compare.10, s32[32]{0:T(128)S(1)} %eq.109), kind=kOutput, calls=%fused_computation.3.clone.1 | convolution fusion | flops 910689792 | bytes 25165952 | tf_op jit(solution)/shard_map/while/body/eval_jaxpr/dot_general | solution.py:92
  323.6 6.9 fusion.57
  333.9 5.3 collective-permute-start.4
  344.3 61.0 %collective-permute-done.4 = f32[1024,768]{1,0:T(8,128)} collective-permute-done((f32[1024,768]{1,0:T(8,128)}, f32[1024,768]{1,0:T(8,128)}, u32[]{:S(2)}, u32[]{:S(2)}) %collective-permute-start.4) | collective-permute-done | bytes 3145760 | tf_op jit(solution)/shard_map/ppermute | solution.py:22
  405.4 9.4 collective-permute-done.5
  414.8 6.0 add_add_fusion.1
  427.7 10.5 %psum.29 = f32[1024]{0:T(1024)S(1)} all-reduce(f32[1024]{0:T(1024)S(1)} %add_add_fusion.3), channel_id=1, replica_groups=mesh['group'=4,'blk'=32] {'group'}, use_global_device_ids=true, to_apply=%region_7.8 | all-reduce | flops 1024 | bytes 8192 | tf_op jit(solution)/shard_map/psum | solution.py:130
  438.2 57.2 %all-reduce.3.cloned.1.call-done = f32[1024,768]{1,0:T(8,128)} async-done(((f32[1024,768]{1,0:T(8,128)}), f32[1024,768]{1,0:T(8,128)}) %all-reduce.3.cloned.1.call-update) | async-done | bytes 3145744 | tf_op jit(solution)/shard_map/psum | solution.py:130
  503.5 5.7 collective-permute-start.11
  509.3 28.5 %collective-permute-done.10 = bf16[1024]{0:T(1024)(128)(2,1)S(1)} collective-permute-done((bf16[1024]{0:T(1024)(128)(2,1)S(1)}, bf16[1024]{0:T(1024)(128)(2,1)S(1)}, u32[]{:S(2)}, u32[]{:S(2)}) %collective-permute-start.10) | collective-permute-done | bytes 2080 | tf_op jit(solution)/shard_map/ppermute | solution.py:32
  542.6 6.9 reshape.99
  549.5 258.4 %while.27 = (s32[]{:T(128)}, f32[48,49152]{1,0:T(8,128)}, f32[48,64]{1,0:T(8,128)S(1)}, s32[8,8,4]{2,1,0:T(8,128)S(1)}, bf16[8,8,128,768]{3,2,1,0:T(8,128)(2,1)}...) while((s32[]{:T(128)}, f32[48,49152]{1,0:T(8,128)}, ...), condition=%wide.region_13.14_spmd.clone, body=%wide.region_9.13_spmd.clone.sunk | while | flops 1873029376 | bytes 67745896 | solution.py:107
  560.1 5.0 fusion.119
  565.1 6.2 reshape.116
  571.3 8.9 convolution_add_fusion.10
  596.2 6.2 reshape.116
  602.4 10.3 %convolution_add_fusion.10 = f32[48,49152]{1,0:T(8,128)} fusion(f32[32,49152]{1,0:T(8,128)} %reshape.116, f32[48,49152]{1,0:T(8,128)} %get-tuple-element.337, pred[]{:T(512)S(6)} %compare.11, s32[32]{0:T(128)S(1)} %eq.118), kind=kOutput, calls=%fused_computation.28.clone.1 | convolution fusion | flops 910689792 | bytes 25165952 | tf_op jit(solution)/shard_map/while/body/eval_jaxpr/dot_general | solution.py:92
  628.7 6.2 reshape.116
  634.9 10.3 %convolution_add_fusion.10 = f32[48,49152]{1,0:T(8,128)} fusion(f32[32,49152]{1,0:T(8,128)} %reshape.116, f32[48,49152]{1,0:T(8,128)} %get-tuple-element.337, pred[]{:T(512)S(6)} %compare.11, s32[32]{0:T(128)S(1)} %eq.118), kind=kOutput, calls=%fused_computation.28.clone.1 | convolution fusion | flops 910689792 | bytes 25165952 | tf_op jit(solution)/shard_map/while/body/eval_jaxpr/dot_general | solution.py:92
  661.1 6.2 reshape.116
  667.3 10.3 %convolution_add_fusion.10 = f32[48,49152]{1,0:T(8,128)} fusion(f32[32,49152]{1,0:T(8,128)} %reshape.116, f32[48,49152]{1,0:T(8,128)} %get-tuple-element.337, pred[]{:T(512)S(6)} %compare.11, s32[32]{0:T(128)S(1)} %eq.118), kind=kOutput, calls=%fused_computation.28.clone.1 | convolution fusion | flops 910689792 | bytes 25165952 | tf_op jit(solution)/shard_map/while/body/eval_jaxpr/dot_general | solution.py:92
  693.6 6.2 reshape.116
  699.8 10.3 %convolution_add_fusion.10 = f32[48,49152]{1,0:T(8,128)} fusion(f32[32,49152]{1,0:T(8,128)} %reshape.116, f32[48,49152]{1,0:T(8,128)} %get-tuple-element.337, pred[]{:T(512)S(6)} %compare.11, s32[32]{0:T(128)S(1)} %eq.118), kind=kOutput, calls=%fused_computation.28.clone.1 | convolution fusion | flops 910689792 | bytes 25165952 | tf_op jit(solution)/shard_map/while/body/eval_jaxpr/dot_general | solution.py:92
  726.1 6.2 reshape.116
  732.3 10.3 %convolution_add_fusion.10 = f32[48,49152]{1,0:T(8,128)} fusion(f32[32,49152]{1,0:T(8,128)} %reshape.116, f32[48,49152]{1,0:T(8,128)} %get-tuple-element.337, pred[]{:T(512)S(6)} %compare.11, s32[32]{0:T(128)S(1)} %eq.118), kind=kOutput, calls=%fused_computation.28.clone.1 | convolution fusion | flops 910689792 | bytes 25165952 | tf_op jit(solution)/shard_map/while/body/eval_jaxpr/dot_general | solution.py:92
  758.6 6.2 reshape.116
  764.8 10.3 %convolution_add_fusion.10 = f32[48,49152]{1,0:T(8,128)} fusion(f32[32,49152]{1,0:T(8,128)} %reshape.116, f32[48,49152]{1,0:T(8,128)} %get-tuple-element.337, pred[]{:T(512)S(6)} %compare.11, s32[32]{0:T(128)S(1)} %eq.118), kind=kOutput, calls=%fused_computation.28.clone.1 | convolution fusion | flops 910689792 | bytes 25165952 | tf_op jit(solution)/shard_map/while/body/eval_jaxpr/dot_general | solution.py:92
  791.1 6.2 reshape.116
  797.3 10.3 %convolution_add_fusion.10 = f32[48,49152]{1,0:T(8,128)} fusion(f32[32,49152]{1,0:T(8,128)} %reshape.116, f32[48,49152]{1,0:T(8,128)} %get-tuple-element.337, pred[]{:T(512)S(6)} %compare.11, s32[32]{0:T(128)S(1)} %eq.118), kind=kOutput, calls=%fused_computation.28.clone.1 | convolution fusion | flops 910689792 | bytes 25165952 | tf_op jit(solution)/shard_map/while/body/eval_jaxpr/dot_general | solution.py:92
  807.9 6.9 fusion.56
  818.2 5.4 collective-permute-start.12
  828.7 61.1 %collective-permute-done.12 = f32[1024,768]{1,0:T(8,128)} collective-permute-done((f32[1024,768]{1,0:T(8,128)}, f32[1024,768]{1,0:T(8,128)}, u32[]{:S(2)}, u32[]{:S(2)}) %collective-permute-start.12) | collective-permute-done | bytes 3145760 | tf_op jit(solution)/shard_map/ppermute | solution.py:22
  889.8 9.4 collective-permute-done.13
  899.3 6.0 add_add_fusion
  912.1 10.4 %psum.31 = f32[1024]{0:T(1024)S(1)} all-reduce(f32[1024]{0:T(1024)S(1)} %add_add_fusion.2), channel_id=1, replica_groups=mesh['group'=4,'blk'=32] {'group'}, use_global_device_ids=true, to_apply=%region_15.16 | all-reduce | flops 1024 | bytes 8192 | tf_op jit(solution)/shard_map/psum | solution.py:130
  923.2 55.3 %all-reduce.5.cloned.1.call-done = f32[1024,768]{1,0:T(8,128)} async-done(((f32[1024,768]{1,0:T(8,128)}), f32[1024,768]{1,0:T(8,128)}) %all-reduce.5.cloned.1.call-update) | async-done | bytes 3145744 | tf_op jit(solution)/shard_map/psum | solution.py:130
  (245 shorter events, 270.0 us)
Async XLA Ops:
  7.2 45.2 %copy-start.2 = (bf16[1024,768]{1,0:T(8,128)(2,1)S(1)}, bf16[1024,768]{1,0:T(8,128)(2,1)}, u32[]{:S(2)}) copy-start(bf16[1024,768]{1,0:T(8,128)(2,1)} %param.10) | copy-start | bytes 4718596
  7.2 488.2 %all-reduce.3.cloned.1.call-start = ((), (), s32[]{:S(2)}) async-start(), calls=%async_computation | async-start | bytes 6291456 | tf_op jit(solution)/shard_map/psum | solution.py:130
  7.2 42.5 %collective-permute-start = (bf16[1024,768]{1,0:T(8,128)(2,1)}, bf16[1024,768]{1,0:T(8,128)(2,1)}, u32[]{:S(2)}, u32[]{:S(2)}) collective-permute-start(bf16[1024,768]{1,0:T(8,128)(2,1)} %param.10), channel_id=1, source_target_pairs={{0,1},{1,2},{2,3},{3,4},{4,5},{5,6},{6,7},{7,8},{8,9},{9,10},{10,1... | collective-permute-start | bytes 4718600 | tf_op jit(solution)/shard_map/ppermute | solution.py:32
  9.3 44.3 %collective-permute-start.1 = (bf16[1024,768]{1,0:T(8,128)(2,1)}, bf16[1024,768]{1,0:T(8,128)(2,1)S(1)}, u32[]{:S(2)}, u32[]{:S(2)}) collective-permute-start(bf16[1024,768]{1,0:T(8,128)(2,1)} %param.10), channel_id=1, source_target_pairs={{1,0},{2,1},{3,2},{4,3},{5,4},{6,5},{7,6},{8,7},{9,8},{10,9},{11,1... | collective-permute-start | bytes 4718600 | tf_op jit(solution)/shard_map/ppermute | solution.py:34
  15.2 34.4 %collective-permute-start.2 = (bf16[1024]{0:T(1024)(128)(2,1)}, bf16[1024]{0:T(1024)(128)(2,1)S(1)}, u32[]{:S(2)}, u32[]{:S(2)}) collective-permute-start(bf16[1024]{0:T(1024)(128)(2,1)} %param.11), channel_id=1, source_target_pairs={{0,1},{1,2},{2,3},{3,4},{4,5},{5,6},{6,7},{7,8},{8,9},{9,10},{10,1... | collective-permute-start | bytes 6152 | tf_op jit(solution)/shard_map/ppermute | solution.py:32
  15.2 34.5 %collective-permute-start.3 = (bf16[1024]{0:T(1024)(128)(2,1)}, bf16[1024]{0:T(1024)(128)(2,1)S(1)}, u32[]{:S(2)}, u32[]{:S(2)}) collective-permute-start(bf16[1024]{0:T(1024)(128)(2,1)} %param.11), channel_id=1, source_target_pairs={{1,0},{2,1},{3,2},{4,3},{5,4},{6,5},{7,6},{8,7},{9,8},{10,9},{11,1... | collective-permute-start | bytes 6152 | tf_op jit(solution)/shard_map/ppermute | solution.py:34
  333.9 71.4 %collective-permute-start.4 = (f32[1024,768]{1,0:T(8,128)}, f32[1024,768]{1,0:T(8,128)}, u32[]{:S(2)}, u32[]{:S(2)}) collective-permute-start(f32[1024,768]{1,0:T(8,128)} %squeeze.47), channel_id=1, source_target_pairs={{1,0},{2,1},{3,2},{4,3},{5,4},{6,5},{7,6},{8,7},{9,8},{10,9},{11,1... | collective-permute-start | bytes 9437192 | tf_op jit(solution)/shard_map/ppermute | solution.py:22
  342.5 72.3 %collective-permute-start.5 = (f32[1024,768]{1,0:T(8,128)}, f32[1024,768]{1,0:T(8,128)}, u32[]{:S(2)}, u32[]{:S(2)}) collective-permute-start(f32[1024,768]{1,0:T(8,128)} %squeeze.48), channel_id=1, source_target_pairs={{31,0},{0,1},{1,2},{2,3},{3,4},{4,5},{5,6},{6,7},{7,8},{8,9},{9,10... | collective-permute-start | bytes 9437192 | tf_op jit(solution)/shard_map/ppermute | solution.py:22
  420.8 17.4 %copy-start.4 = (bf16[1024]{0:T(1024)(128)(2,1)S(1)}, bf16[1024]{0:T(1024)(128)(2,1)}, u32[]{:S(2)}) copy-start(bf16[1024]{0:T(1024)(128)(2,1)} %param.11) | copy-start | bytes 6148
  420.8 74.7 %copy-start.3 = (bf16[1024,768]{1,0:T(8,128)(2,1)S(1)}, bf16[1024,768]{1,0:T(8,128)(2,1)}, u32[]{:S(2)}) copy-start(bf16[1024,768]{1,0:T(8,128)(2,1)} %param.10) | copy-start | bytes 4718596
  420.8 557.7 %all-reduce.5.cloned.1.call-start = ((), (), s32[]{:S(2)}) async-start(), calls=%async_computation.1 | async-start | bytes 6291456 | tf_op jit(solution)/shard_map/psum | solution.py:130
  420.9 2.5 collective-permute-start.6
  421.0 6.7 collective-permute-start.7
  497.7 44.8 %copy-start = (bf16[1024,768]{1,0:T(8,128)(2,1)}, bf16[1024,768]{1,0:T(8,128)(2,1)S(1)}, u32[]{:S(2)}) copy-start(bf16[1024,768]{1,0:T(8,128)(2,1)S(1)} %divide_convert_fusion.3) | copy-start | bytes 4718596
  497.7 40.2 %collective-permute-start.8 = (bf16[1024,768]{1,0:T(8,128)(2,1)S(1)}, bf16[1024,768]{1,0:T(8,128)(2,1)S(1)}, u32[]{:S(2)}, u32[]{:S(2)}) collective-permute-start(bf16[1024,768]{1,0:T(8,128)(2,1)S(1)} %divide_convert_fusion.3), channel_id=1, source_target_pairs={{0,1},{1,2},{2,3},{3,4},{4,5},{5,6},{6,7},{7,8},{8,9},{9,10},{10,1... | collective-permute-start | bytes 4718600 | tf_op jit(solution)/shard_map/ppermute | solution.py:32
  499.0 38.9 %collective-permute-start.9 = (bf16[1024,768]{1,0:T(8,128)(2,1)S(1)}, bf16[1024,768]{1,0:T(8,128)(2,1)}, u32[]{:S(2)}, u32[]{:S(2)}) collective-permute-start(bf16[1024,768]{1,0:T(8,128)(2,1)S(1)} %divide_convert_fusion.3), channel_id=1, source_target_pairs={{1,0},{2,1},{3,2},{4,3},{5,4},{6,5},{7,6},{8,7},{9,8},{10,9},{11,1... | collective-permute-start | bytes 4718600 | tf_op jit(solution)/shard_map/ppermute | solution.py:34
  503.5 34.3 %collective-permute-start.10 = (bf16[1024]{0:T(1024)(128)(2,1)S(1)}, bf16[1024]{0:T(1024)(128)(2,1)S(1)}, u32[]{:S(2)}, u32[]{:S(2)}) collective-permute-start(bf16[1024]{0:T(1024)(128)(2,1)S(1)} %get-tuple-element.196), channel_id=1, source_target_pairs={{0,1},{1,2},{2,3},{3,4},{4,5},{5,6},{6,7},{7,8},{8,9},{9,10},{10,1... | collective-permute-start | bytes 6152 | tf_op jit(solution)/shard_map/ppermute | solution.py:32
  503.5 34.3 %collective-permute-start.11 = (bf16[1024]{0:T(1024)(128)(2,1)S(1)}, bf16[1024]{0:T(1024)(128)(2,1)S(1)}, u32[]{:S(2)}, u32[]{:S(2)}) collective-permute-start(bf16[1024]{0:T(1024)(128)(2,1)S(1)} %get-tuple-element.196), channel_id=1, source_target_pairs={{1,0},{2,1},{3,2},{4,3},{5,4},{6,5},{7,6},{8,7},{9,8},{10,9},{11,1... | collective-permute-start | bytes 6152 | tf_op jit(solution)/shard_map/ppermute | solution.py:34
  818.2 71.7 %collective-permute-start.12 = (f32[1024,768]{1,0:T(8,128)}, f32[1024,768]{1,0:T(8,128)}, u32[]{:S(2)}, u32[]{:S(2)}) collective-permute-start(f32[1024,768]{1,0:T(8,128)} %squeeze.53), channel_id=1, source_target_pairs={{1,0},{2,1},{3,2},{4,3},{5,4},{6,5},{7,6},{8,7},{9,8},{10,9},{11,1... | collective-permute-start | bytes 9437192 | tf_op jit(solution)/shard_map/ppermute | solution.py:22
  826.8 72.4 %collective-permute-start.13 = (f32[1024,768]{1,0:T(8,128)}, f32[1024,768]{1,0:T(8,128)}, u32[]{:S(2)}, u32[]{:S(2)}) collective-permute-start(f32[1024,768]{1,0:T(8,128)} %squeeze.54), channel_id=1, source_target_pairs={{31,0},{0,1},{1,2},{2,3},{3,4},{4,5},{5,6},{6,7},{7,8},{8,9},{9,10... | collective-permute-start | bytes 9437192 | tf_op jit(solution)/shard_map/ppermute | solution.py:22
  905.2 73.2 %copy-start.1 = (bf16[1024,768]{1,0:T(8,128)(2,1)S(1)}, bf16[1024,768]{1,0:T(8,128)(2,1)}, u32[]{:S(2)}) copy-start(bf16[1024,768]{1,0:T(8,128)(2,1)} %copy-done) | copy-start | bytes 4718596
  905.3 2.5 collective-permute-start.14
  905.4 6.7 collective-permute-start.15
Sparse Core Ops, SparseCore 0:
  420.9 74.4 all-reduce.2
  905.4 73.0 all-reduce.4
where the time goes:
time: 991 us; the launch traced here: 989 us
  matrix products  363 us (37%)
  waiting for transfers between devices  320 us (32%)
  local copies, waits for them, and re-layouts  201 us (20%)
  starting transfers between devices  38.7 us (4%)
  other arithmetic  30.6 us (3%)
  blocking collectives  20.9 us (2%)
  between operations  14.2 us (1%)
    dot_general x16, matrix products, tile_step(): jnp.dot(picker_f.T, numerator, precision=lax.Precision.HIGHEST, preferred...  162 us
    ppermute x8, waiting for transfers between devices, passed_along(): return lax.ppermute(block, axis, route)  151 us
    psum x2, waiting for transfers between devices, per_device(): total_num, total_mass = lax.psum((own_num, own_mass), 'group')  113 us
    reshape x16, local copies, waits for them, and re-layouts, tile_step(): numerator = numerator.reshape(group_size * SLOTS, BLOCK * width)  99.3 us
    dot_general x16, matrix products, tile_step(): jnp.einsum('tpk,tpd->tkd', membership, tile_points, preferred_element_typ...  80.8 us
    sub x16, matrix products, tile_step(): membership = jax.nn.softmax(scores, axis=-1).astype(jnp.bfloat16)  59.2 us
    ppermute x4, waiting for transfers between devices, with_halo(): lax.ppermute(tail, axis, [(i, (i + 1) % count) for i in range(count)])  55.7 us
    dot_general x16, matrix products, tile_step(): jnp.dot(picker.astype(jnp.bfloat16), cand_flat, preferred_element_type=jn...  53.8 us
  transfers between devices with their start and end apart: 18, of which 12 were waited for; matrix products, arithmetic and copies ran while one was open for 2% of the time, Pallas kernels for 0%

commit v1 on v0

--- a/solution.py
+++ b/solution.py
@@ -1,8 +1,10 @@
-import math
+import functools
 
 import jax
 import jax.numpy as jnp
 from jax import lax
+from jax.experimental import pallas as pl
+from jax.experimental.pallas import tpu as pltpu
 from jax.sharding import PartitionSpec as P
 
 D = 768
@@ -53,59 +55,71 @@
     return (near_num[1] + upper_num + lower_num, near_mass[1] + upper_mass + lower_mass)
 
 
+def tile_kernel(ids_ref, pts_ref, cand_ref, off_ref, num_ref, mass_ref):
+    t = pl.program_id(0)
+
+    @pl.when(t == 0)
+    def _():
+        num_ref[...] = jnp.zeros_like(num_ref)
+        mass_ref[...] = jnp.zeros_like(mass_ref)
+
+    x = pts_ref[...]
+    ids = [ids_ref[t, s] for s in range(SLOTS)]
+    cands = jnp.concatenate([cand_ref[i] for i in ids], axis=0)
+    offs = jnp.concatenate([off_ref[i] for i in ids], axis=1)
+    scores = lax.dot_general(
+        x, cands, (((1,), (1,)), ((), ())), preferred_element_type=jnp.float32
+    ) * (32.0 / D)
+    scores = scores + offs
+    top = jnp.max(scores, axis=-1, keepdims=True)
+    unnorm = jnp.exp(scores - top)
+    member = (unnorm / jnp.sum(unnorm, axis=-1, keepdims=True)).astype(jnp.bfloat16)
+    mass = jnp.sum(member.astype(jnp.float32), axis=0, keepdims=True)
+    num = lax.dot_general(
+        member, x, (((0,), (0,)), ((), ())), preferred_element_type=jnp.float32
+    )
+    for s in range(SLOTS):
+        i = ids[s]
+        num_ref[i] += num[s * BLOCK:(s + 1) * BLOCK]
+        mass_ref[i] += mass[:, s * BLOCK:(s + 1) * BLOCK]
+
+
 def assign_tiles(points, near_ids, near_centroids, offsets):
     tile_count = near_ids.shape[0]
-    group_size = math.gcd(tile_count, 8)
+    width = points.shape[1]
     block_total = near_centroids.shape[0] // BLOCK
-    width = points.shape[1]
-    cand_flat = near_centroids.reshape(block_total, BLOCK * width)
-    offset_blocks = offsets.reshape(block_total, BLOCK)
-    tiled_points = points.reshape(tile_count // group_size, group_size, TILE, width)
-    tiled_ids = near_ids.reshape(tile_count // group_size, group_size, SLOTS)
-    block_iota = jnp.arange(block_total, dtype=jnp.int32)
-
-    def tile_step(running, packet):
-        sum_num, sum_mass = running
-        tile_points, block_ids = packet
-        picker = block_ids.reshape(-1)[:, None] == block_iota[None, :]
-        candidates = jnp.dot(
-            picker.astype(jnp.bfloat16), cand_flat, preferred_element_type=jnp.float32
-        ).astype(jnp.bfloat16)
-        candidates = candidates.reshape(group_size, SLOTS * BLOCK, width)
-        picker_f = picker.astype(jnp.float32)
-        cand_offsets = jnp.dot(
-            picker_f,
-            offset_blocks,
-            precision=lax.Precision.HIGHEST,
-            preferred_element_type=jnp.float32,
-        )
-        scores = jnp.einsum(
-            "tpd,tkd->tpk", tile_points, candidates, preferred_element_type=jnp.float32
-        ) * (32.0 / width)
-        scores = scores + cand_offsets.reshape(group_size, 1, SLOTS * BLOCK)
-        membership = jax.nn.softmax(scores, axis=-1).astype(jnp.bfloat16)
-        masses = jnp.sum(membership.astype(jnp.float32), axis=1).reshape(group_size * SLOTS, BLOCK)
-        numerator = jnp.einsum(
-            "tpk,tpd->tkd", membership, tile_points, preferred_element_type=jnp.float32
-        )
-        numerator = numerator.reshape(group_size * SLOTS, BLOCK * width)
-        add_num = jnp.dot(
-            picker_f.T,
-            numerator,
-            precision=lax.Precision.HIGHEST,
-            preferred_element_type=jnp.float32,
-        )
-        add_mass = jnp.dot(
-            picker_f.T, masses, precision=lax.Precision.HIGHEST, preferred_element_type=jnp.float32
-        )
-        return ((sum_num + add_num, sum_mass + add_mass), None)
-
-    start = (
-        jnp.zeros((block_total, BLOCK * width), jnp.float32),
-        jnp.zeros((block_total, BLOCK), jnp.float32),
-    )
-    (sum_num, sum_mass), _ = lax.scan(tile_step, start, (tiled_points, tiled_ids))
-    return (sum_num.reshape(3, -1, width), sum_mass.reshape(3, -1))
+    cand = near_centroids.reshape(block_total, BLOCK, width)
+    off = offsets.reshape(block_total, 1, BLOCK)
+    flops = 4 * tile_count * TILE * SLOTS * BLOCK * width
+    num, mass = pl.pallas_call(
+        tile_kernel,
+        out_shape=(
+            jax.ShapeDtypeStruct((block_total, BLOCK, width), jnp.float32),
+            jax.ShapeDtypeStruct((block_total, 1, BLOCK), jnp.float32),
+        ),
+        grid_spec=pltpu.PrefetchScalarGridSpec(
+            num_scalar_prefetch=1,
+            grid=(tile_count,),
+            in_specs=[
+                pl.BlockSpec((TILE, width), lambda t, ids: (t, 0)),
+                pl.BlockSpec((block_total, BLOCK, width), lambda t, ids: (0, 0, 0)),
+                pl.BlockSpec((block_total, 1, BLOCK), lambda t, ids: (0, 0, 0)),
+            ],
+            out_specs=[
+                pl.BlockSpec((block_total, BLOCK, width), lambda t, ids: (0, 0, 0)),
+                pl.BlockSpec((block_total, 1, BLOCK), lambda t, ids: (0, 0, 0)),
+            ],
+        ),
+        compiler_params=pltpu.CompilerParams(
+            dimension_semantics=("arbitrary",), vmem_limit_bytes=56 * 1024 * 1024
+        ),
+        cost_estimate=pl.CostEstimate(
+            flops=flops,
+            transcendentals=tile_count * TILE * SLOTS * BLOCK,
+            bytes_accessed=points.size * 2 + cand.size * 2 + block_total * BLOCK * width * 4,
+        ),
+    )(near_ids, points, cand, off)
+    return (num.reshape(3, -1, width), mass.reshape(3, -1))
 
 
 def per_device(points, block_lists, centroids, dual_weights):

time: 991 us -> 567 us (0.57)
  matrix products: 363 us -> 0 us
  local copies, waits for them, and re-layouts: 201 us -> 17.6 us
  Pallas kernels: 0 us -> 133 us
  other arithmetic: 30.6 us -> 18.6 us
    dot_general x80 -> x0, matrix products: 304 us -> none  [the longest x16 162 us: tile_step(): jnp.dot(picker_f.T, numerator, precision=lax.Precision.HIGHEST, preferred...]
    reshape x50 -> x0, local copies, waits for them, and re-layouts: 161 us -> none  [the longest x16 99.3 us: tile_step(): numerator = numerator.reshape(group_size * SLOTS, BLOCK * width)]
    pallas_call x0 -> x2, Pallas kernels: none -> 133 us  [assign_tiles(): pl.pallas_call(tile_kernel, out_shape=(jax.ShapeDtypeStruct((block_total,...]
    sub x16 -> x0, matrix products: 59.2 us -> none  [tile_step(): membership = jax.nn.softmax(scores, axis=-1).astype(jnp.bfloat16)]
    slice x4 -> x2, local copies, waits for them, and re-layouts: 13.9 us -> 0.13 us  [return_cycle(): upper_num, upper_mass = passed_along((near_num[0], near_mass[0]), 'blk', -1)]
  transfers between devices with their start and end apart: 18 -> 18, of which waited for: 12 -> 12; matrix products, arithmetic and copies ran while one was open for 2% -> 1% of each run, Pallas kernels for 0% -> 0%
where the time goes in v1:
time: 567 us; the launch traced here: 564 us
  waiting for transfers between devices  321 us (57%)
  Pallas kernels  133 us (23%)
  starting transfers between devices  39.1 us (7%)
  blocking collectives  20.9 us (4%)
  other arithmetic  18.6 us (3%)
  local copies, waits for them, and re-layouts  17.6 us (3%)
  between operations  14.2 us (3%)
    ppermute x8, waiting for transfers between devices, passed_along(): return lax.ppermute(block, axis, route)  155 us
    pallas_call x2, Pallas kernels, assign_tiles(): pl.pallas_call(tile_kernel, out_shape=(jax.ShapeDtypeStruct((block_total,...  133 us
    psum x2, waiting for transfers between devices, per_device(): total_num, total_mass = lax.psum((own_num, own_mass), 'group')  111 us
    ppermute x4, waiting for transfers between devices, with_halo(): lax.ppermute(tail, axis, [(i, (i + 1) % count) for i in range(count)])  55 us
    ppermute x4, starting transfers between devices, with_halo(): lax.ppermute(head, axis, [((i + 1) % count, i) for i in range(count)])  21.7 us
    psum x2, blocking collectives, per_device(): total_num, total_mass = lax.psum((own_num, own_mass), 'group')  20.9 us
    ppermute x8, starting transfers between devices, passed_along(): return lax.ppermute(block, axis, route)  13.9 us
  transfers between devices with their start and end apart: 18, of which 12 were waited for; matrix products, arithmetic and copies ran while one was open for 1% of the time, Pallas kernels for 0%

profile of v1, /device:TPU:1, one launch (start us, length us, event | category | flops | bytes accessed | tf_op | source)
XLA Modules:
  0.0 564.2 jit_solution(4600607773654579977)
XLA Ops:
  7.2 2.1 collective-permute-start
  9.3 5.8 %collective-permute-start.1 = (bf16[1024,768]{1,0:T(8,128)(2,1)}, bf16[1024,768]{1,0:T(8,128)(2,1)S(1)}, u32[]{:S(2)}, u32[]{:S(2)}) collective-permute-start(bf16[1024,768]{1,0:T(8,128)(2,1)} %param.6), channel_id=1, source_target_pairs={{1,0},{2,1},{3,2},{4,3},{5,4},{6,5},{7,6},{8,7},{9,8},{10,9},{11,1... | collective-permute-start | bytes 4718600 | tf_op jit(solution)/shard_map/ppermute | solution.py:36
  15.2 5.7 %collective-permute-start.3 = (bf16[1024]{0:T(1024)(128)(2,1)}, bf16[1024]{0:T(1024)(128)(2,1)S(1)}, u32[]{:S(2)}, u32[]{:S(2)}) collective-permute-start(bf16[1024]{0:T(1024)(128)(2,1)} %param.7), channel_id=1, source_target_pairs={{1,0},{2,1},{3,2},{4,3},{5,4},{6,5},{7,6},{8,7},{9,8},{10,9},{11,1... | collective-permute-start | bytes 6152 | tf_op jit(solution)/shard_map/ppermute | solution.py:36
  20.9 0.8 copy.10
  21.6 0.7 fusion.6.ids_ref
  22.3 0.8 concatenate.49
  23.0 26.5 %collective-permute-done.2 = bf16[1024]{0:T(1024)(128)(2,1)S(1)} collective-permute-done((bf16[1024]{0:T(1024)(128)(2,1)}, bf16[1024]{0:T(1024)(128)(2,1)S(1)}, u32[]{:S(2)}, u32[]{:S(2)}) %collective-permute-start.2) | collective-permute-done | bytes 2080 | tf_op jit(solution)/shard_map/ppermute | solution.py:34
  49.6 0.1 concatenate.48
  49.6 0.1 concatenate.50
  49.7 1.5 constant_dynamic-update-slice_fusion.2
  51.3 0.1 constant_dynamic-update-slice_fusion.1
  51.4 0.1 constant_dynamic-update-slice_fusion
  51.5 2.2 copy-done
  53.7 1.0 multiply_reduce_fusion.1
  54.7 0.1 mul.38
  54.8 0.7 fusion.8.off_ref
  55.5 66.6 %shard_map.59 = (f32[48,64,768]{2,1,0:T(8,128)}, f32[48,1,64]{2,1,0:T(1,128)}) custom-call(s32[64,4]{1,0:T(8,128)} %fusion.6.ids_ref, bf16[8192,768]{1,0:T(8,128)(2,1)} %pts_ref.3, bf16[48,64,768]{2,1,0:T(8,128)(2,1)} %bitcast.14, f32[48,1,64]{2,1,0:T(1,128)} %fusion.8.off_ref), custom_call_target="tpu_custom_call" | custom-call | flops 6442450944 | bytes 26738688 | tf_op jit(solution)/shard_map/pallas_call | solution.py:94
  122.1 4.8 fusion.11
  127.0 5.3 collective-permute-start.4
  132.3 65.8 %collective-permute-done.4 = f32[1024,768]{1,0:T(8,128)S(1)} collective-permute-done((f32[1024,768]{1,0:T(8,128)S(1)}, f32[1024,768]{1,0:T(8,128)S(1)}, u32[]{:S(2)}, u32[]{:S(2)}) %collective-permute-start.4) | collective-permute-done | bytes 3145760 | tf_op jit(solution)/shard_map/ppermute | solution.py:24
  198.1 6.1 %collective-permute-done.5 = f32[1024,768]{1,0:T(8,128)S(1)} collective-permute-done((f32[1024,768]{1,0:T(8,128)S(1)}, f32[1024,768]{1,0:T(8,128)S(1)}, u32[]{:S(2)}, u32[]{:S(2)}) %collective-permute-start.5) | collective-permute-done | bytes 3145760 | tf_op jit(solution)/shard_map/ppermute | solution.py:24
  204.3 2.3 fusion.1
  206.6 0.0 all-reduce.5.cloned.1.call-start
  206.6 0.7 copy-done.2
  207.3 0.1 slice_reduce_fusion.4
  207.4 0.1 squeeze.40
  207.4 0.3 collective-permute-start.6
  207.7 0.1 squeeze.41
  207.8 1.2 collective-permute-start.7
  209.0 0.1 squeeze.39
  209.1 0.9 collective-permute-done.6
  209.9 4.6 collective-permute-done.7
  214.5 10.5 %psum.29 = f32[1024]{0:T(1024)S(1)} all-reduce(f32[1024]{0:T(1024)S(1)} %add_add_fusion.1), channel_id=1, replica_groups=mesh['group'=4,'blk'=32] {'group'}, use_global_device_ids=true, to_apply=%region_2.3 | all-reduce | flops 1024 | bytes 8192 | tf_op jit(solution)/shard_map/psum | solution.py:144
  225.0 56.3 %all-reduce.3.cloned.1.call-done = f32[1024,768]{1,0:T(8,128)} async-done(((f32[1024,768]{1,0:T(8,128)}), f32[1024,768]{1,0:T(8,128)}) %all-reduce.3.cloned.1.call-update) | async-done | bytes 3145744 | tf_op jit(solution)/shard_map/psum | solution.py:144
  281.2 2.3 divide_convert_fusion.1
  283.5 1.3 collective-permute-start.8
  284.8 4.5 collective-permute-start.9
  289.3 5.7 %collective-permute-start.11 = (bf16[1024]{0:T(1024)(128)(2,1)S(1)}, bf16[1024]{0:T(1024)(128)(2,1)S(1)}, u32[]{:S(2)}, u32[]{:S(2)}) collective-permute-start(bf16[1024]{0:T(1024)(128)(2,1)S(1)} %get-tuple-element.26), channel_id=1, source_target_pairs={{1,0},{2,1},{3,2},{4,3},{5,4},{6,5},{7,6},{8,7},{9,8},{10,9},{11,1... | collective-permute-start | bytes 6152 | tf_op jit(solution)/shard_map/ppermute | solution.py:36
  295.0 0.1 concatenate.52
  295.1 28.5 %collective-permute-done.10 = bf16[1024]{0:T(1024)(128)(2,1)S(1)} collective-permute-done((bf16[1024]{0:T(1024)(128)(2,1)S(1)}, bf16[1024]{0:T(1024)(128)(2,1)S(1)}, u32[]{:S(2)}, u32[]{:S(2)}) %collective-permute-start.10) | collective-permute-done | bytes 2080 | tf_op jit(solution)/shard_map/ppermute | solution.py:34
  323.6 0.1 concatenate.51
  323.6 0.1 concatenate.53
  323.7 4.7 multiply_reduce_fusion
  328.4 0.1 mul.41
  328.5 0.7 fusion.9.off_ref
  329.2 66.6 %shard_map.60 = (f32[48,64,768]{2,1,0:T(8,128)}, f32[48,1,64]{2,1,0:T(1,128)}) custom-call(s32[64,4]{1,0:T(8,128)} %fusion.6.ids_ref, bf16[8192,768]{1,0:T(8,128)(2,1)} %pts_ref.3, bf16[48,64,768]{2,1,0:T(8,128)(2,1)} %bitcast.15, f32[48,1,64]{2,1,0:T(1,128)} %fusion.9.off_ref), custom_call_target="tpu_custom_call" | custom-call | flops 6442450944 | bytes 26738688 | tf_op jit(solution)/shard_map/pallas_call | solution.py:94
  395.8 4.8 fusion.10
  400.6 5.6 collective-permute-start.12
  406.3 66.0 %collective-permute-done.12 = f32[1024,768]{1,0:T(8,128)S(1)} collective-permute-done((f32[1024,768]{1,0:T(8,128)S(1)}, f32[1024,768]{1,0:T(8,128)S(1)}, u32[]{:S(2)}, u32[]{:S(2)}) %collective-permute-start.12) | collective-permute-done | bytes 3145760 | tf_op jit(solution)/shard_map/ppermute | solution.py:24
  472.3 6.1 %collective-permute-done.13 = f32[1024,768]{1,0:T(8,128)S(1)} collective-permute-done((f32[1024,768]{1,0:T(8,128)S(1)}, f32[1024,768]{1,0:T(8,128)S(1)}, u32[]{:S(2)}, u32[]{:S(2)}) %collective-permute-start.13) | collective-permute-done | bytes 3145760 | tf_op jit(solution)/shard_map/ppermute | solution.py:24
  478.4 2.3 fusion
  480.7 0.7 copy-done.3
  481.4 0.1 slice_reduce_fusion.1
  481.5 0.1 squeeze.46
  481.6 0.3 collective-permute-start.14
  481.9 0.1 squeeze.47
  481.9 1.2 collective-permute-start.15
  483.1 0.1 squeeze.45
  483.2 0.9 collective-permute-done.14
  484.0 4.6 collective-permute-done.15
  488.6 10.4 %psum.31 = f32[1024]{0:T(1024)S(1)} all-reduce(f32[1024]{0:T(1024)S(1)} %add_add_fusion), channel_id=1, replica_groups=mesh['group'=4,'blk'=32] {'group'}, use_global_device_ids=true, to_apply=%region_5.6 | all-reduce | flops 1024 | bytes 8192 | tf_op jit(solution)/shard_map/psum | solution.py:144
  499.0 0.6 add_convert_fusion
  499.6 54.3 %all-reduce.5.cloned.1.call-done = f32[1024,768]{1,0:T(8,128)} async-done(((f32[1024,768]{1,0:T(8,128)}), f32[1024,768]{1,0:T(8,128)}) %all-reduce.5.cloned.1.call-update) | async-done | bytes 3145744 | tf_op jit(solution)/shard_map/psum | solution.py:144
  553.9 3.4 divide_convert_fusion
  (25 shorter events, 0.1 us)
Async XLA Ops:
  7.2 44.1 %copy-start.1 = (bf16[1024,768]{1,0:T(8,128)(2,1)S(1)}, bf16[1024,768]{1,0:T(8,128)(2,1)}, u32[]{:S(2)}) copy-start(bf16[1024,768]{1,0:T(8,128)(2,1)} %param.6) | copy-start | bytes 4718596
  7.2 274.1 %all-reduce.3.cloned.1.call-start = ((), (), s32[]{:S(2)}) async-start(), calls=%async_computation | async-start | bytes 6291456 | tf_op jit(solution)/shard_map/psum | solution.py:144
  7.2 42.5 %collective-permute-start = (bf16[1024,768]{1,0:T(8,128)(2,1)}, bf16[1024,768]{1,0:T(8,128)(2,1)}, u32[]{:S(2)}, u32[]{:S(2)}) collective-permute-start(bf16[1024,768]{1,0:T(8,128)(2,1)} %param.6), channel_id=1, source_target_pairs={{0,1},{1,2},{2,3},{3,4},{4,5},{5,6},{6,7},{7,8},{8,9},{9,10},{10,1... | collective-permute-start | bytes 4718600 | tf_op jit(solution)/shard_map/ppermute | solution.py:34
  9.3 42.0 %collective-permute-start.1 = (bf16[1024,768]{1,0:T(8,128)(2,1)}, bf16[1024,768]{1,0:T(8,128)(2,1)S(1)}, u32[]{:S(2)}, u32[]{:S(2)}) collective-permute-start(bf16[1024,768]{1,0:T(8,128)(2,1)} %param.6), channel_id=1, source_target_pairs={{1,0},{2,1},{3,2},{4,3},{5,4},{6,5},{7,6},{8,7},{9,8},{10,9},{11,1... | collective-permute-start | bytes 4718600 | tf_op jit(solution)/shard_map/ppermute | solution.py:36
  15.2 34.4 %collective-permute-start.2 = (bf16[1024]{0:T(1024)(128)(2,1)}, bf16[1024]{0:T(1024)(128)(2,1)S(1)}, u32[]{:S(2)}, u32[]{:S(2)}) collective-permute-start(bf16[1024]{0:T(1024)(128)(2,1)} %param.7), channel_id=1, source_target_pairs={{0,1},{1,2},{2,3},{3,4},{4,5},{5,6},{6,7},{7,8},{8,9},{9,10},{10,1... | collective-permute-start | bytes 6152 | tf_op jit(solution)/shard_map/ppermute | solution.py:34
  15.2 34.5 %collective-permute-start.3 = (bf16[1024]{0:T(1024)(128)(2,1)}, bf16[1024]{0:T(1024)(128)(2,1)S(1)}, u32[]{:S(2)}, u32[]{:S(2)}) collective-permute-start(bf16[1024]{0:T(1024)(128)(2,1)} %param.7), channel_id=1, source_target_pairs={{1,0},{2,1},{3,2},{4,3},{5,4},{6,5},{7,6},{8,7},{9,8},{10,9},{11,1... | collective-permute-start | bytes 6152 | tf_op jit(solution)/shard_map/ppermute | solution.py:36
  51.5 2.2 copy-start
  127.0 71.2 %collective-permute-start.4 = (f32[1024,768]{1,0:T(8,128)S(1)}, f32[1024,768]{1,0:T(8,128)S(1)}, u32[]{:S(2)}, u32[]{:S(2)}) collective-permute-start(f32[1024,768]{1,0:T(8,128)S(1)} %bitcast.18), channel_id=1, source_target_pairs={{1,0},{2,1},{3,2},{4,3},{5,4},{6,5},{7,6},{8,7},{9,8},{10,9},{11,1... | collective-permute-start | bytes 9437192 | tf_op jit(solution)/shard_map/ppermute | solution.py:24
  132.3 72.0 %collective-permute-start.5 = (f32[1024,768]{1,0:T(8,128)S(1)}, f32[1024,768]{1,0:T(8,128)S(1)}, u32[]{:S(2)}, u32[]{:S(2)}) collective-permute-start(f32[1024,768]{1,0:T(8,128)S(1)} %bitcast.16), channel_id=1, source_target_pairs={{31,0},{0,1},{1,2},{2,3},{3,4},{4,5},{5,6},{6,7},{7,8},{8,9},{9,10... | collective-permute-start | bytes 9437192 | tf_op jit(solution)/shard_map/ppermute | solution.py:24
  206.6 0.7 copy-start.2
  206.6 18.4 %copy-start.4 = (bf16[1024]{0:T(1024)(128)(2,1)S(1)}, bf16[1024]{0:T(1024)(128)(2,1)}, u32[]{:S(2)}) copy-start(bf16[1024]{0:T(1024)(128)(2,1)} %param.7) | copy-start | bytes 6148
  206.6 347.3 %all-reduce.5.cloned.1.call-start = ((), (), s32[]{:S(2)}) async-start(), calls=%async_computation.1 | async-start | bytes 6291456 | tf_op jit(solution)/shard_map/psum | solution.py:144
  207.4 2.5 collective-permute-start.6
  207.8 6.7 %collective-permute-start.7 = (f32[1024]{0:T(1024)S(1)}, f32[1024]{0:T(1024)S(1)}, u32[]{:S(2)}, u32[]{:S(2)}) collective-permute-start(f32[1024]{0:T(1024)S(1)} %squeeze.41), channel_id=1, source_target_pairs={{31,0},{0,1},{1,2},{2,3},{3,4},{4,5},{5,6},{6,7},{7,8},{8,9},{9,10... | collective-permute-start | bytes 12296 | tf_op jit(solution)/shard_map/ppermute | solution.py:24
  283.5 40.2 %collective-permute-start.8 = (bf16[1024,768]{1,0:T(8,128)(2,1)S(1)}, bf16[1024,768]{1,0:T(8,128)(2,1)S(1)}, u32[]{:S(2)}, u32[]{:S(2)}) collective-permute-start(bf16[1024,768]{1,0:T(8,128)(2,1)S(1)} %divide_convert_fusion.1), channel_id=1, source_target_pairs={{0,1},{1,2},{2,3},{3,4},{4,5},{5,6},{6,7},{7,8},{8,9},{9,10},{10,1... | collective-permute-start | bytes 4718600 | tf_op jit(solution)/shard_map/ppermute | solution.py:34
  284.8 38.9 %collective-permute-start.9 = (bf16[1024,768]{1,0:T(8,128)(2,1)S(1)}, bf16[1024,768]{1,0:T(8,128)(2,1)}, u32[]{:S(2)}, u32[]{:S(2)}) collective-permute-start(bf16[1024,768]{1,0:T(8,128)(2,1)S(1)} %divide_convert_fusion.1), channel_id=1, source_target_pairs={{1,0},{2,1},{3,2},{4,3},{5,4},{6,5},{7,6},{8,7},{9,8},{10,9},{11,1... | collective-permute-start | bytes 4718600 | tf_op jit(solution)/shard_map/ppermute | solution.py:36
  289.3 34.3 %collective-permute-start.10 = (bf16[1024]{0:T(1024)(128)(2,1)S(1)}, bf16[1024]{0:T(1024)(128)(2,1)S(1)}, u32[]{:S(2)}, u32[]{:S(2)}) collective-permute-start(bf16[1024]{0:T(1024)(128)(2,1)S(1)} %get-tuple-element.26), channel_id=1, source_target_pairs={{0,1},{1,2},{2,3},{3,4},{4,5},{5,6},{6,7},{7,8},{8,9},{9,10},{10,1... | collective-permute-start | bytes 6152 | tf_op jit(solution)/shard_map/ppermute | solution.py:34
  289.3 34.3 %collective-permute-start.11 = (bf16[1024]{0:T(1024)(128)(2,1)S(1)}, bf16[1024]{0:T(1024)(128)(2,1)S(1)}, u32[]{:S(2)}, u32[]{:S(2)}) collective-permute-start(bf16[1024]{0:T(1024)(128)(2,1)S(1)} %get-tuple-element.26), channel_id=1, source_target_pairs={{1,0},{2,1},{3,2},{4,3},{5,4},{6,5},{7,6},{8,7},{9,8},{10,9},{11,1... | collective-permute-start | bytes 6152 | tf_op jit(solution)/shard_map/ppermute | solution.py:36
  400.6 71.6 %collective-permute-start.12 = (f32[1024,768]{1,0:T(8,128)S(1)}, f32[1024,768]{1,0:T(8,128)S(1)}, u32[]{:S(2)}, u32[]{:S(2)}) collective-permute-start(f32[1024,768]{1,0:T(8,128)S(1)} %bitcast.19), channel_id=1, source_target_pairs={{1,0},{2,1},{3,2},{4,3},{5,4},{6,5},{7,6},{8,7},{9,8},{10,9},{11,1... | collective-permute-start | bytes 9437192 | tf_op jit(solution)/shard_map/ppermute | solution.py:24
  406.3 72.1 %collective-permute-start.13 = (f32[1024,768]{1,0:T(8,128)S(1)}, f32[1024,768]{1,0:T(8,128)S(1)}, u32[]{:S(2)}, u32[]{:S(2)}) collective-permute-start(f32[1024,768]{1,0:T(8,128)S(1)} %bitcast.17), channel_id=1, source_target_pairs={{31,0},{0,1},{1,2},{2,3},{3,4},{4,5},{5,6},{6,7},{7,8},{8,9},{9,10... | collective-permute-start | bytes 9437192 | tf_op jit(solution)/shard_map/ppermute | solution.py:24
  480.7 0.7 copy-start.3
  481.6 2.5 collective-permute-start.14
  481.9 6.7 %collective-permute-start.15 = (f32[1024]{0:T(1024)S(1)}, f32[1024]{0:T(1024)S(1)}, u32[]{:S(2)}, u32[]{:S(2)}) collective-permute-start(f32[1024]{0:T(1024)S(1)} %squeeze.47), channel_id=1, source_target_pairs={{31,0},{0,1},{1,2},{2,3},{3,4},{4,5},{5,6},{6,7},{7,8},{8,9},{9,10... | collective-permute-start | bytes 12296 | tf_op jit(solution)/shard_map/ppermute | solution.py:24
Sparse Core Ops, SparseCore 0:
  206.7 74.4 all-reduce.2
  480.8 73.0 all-reduce.4

commit v2 on v1

--- a/solution.py
+++ b/solution.py
@@ -55,7 +55,7 @@
     return (near_num[1] + upper_num + lower_num, near_mass[1] + upper_mass + lower_mass)
 
 
-def tile_kernel(ids_ref, pts_ref, cand_ref, off_ref, num_ref, mass_ref):
+def tile_kernel(per_step, ids_ref, pts_ref, cand_ref, off_ref, num_ref, mass_ref):
     t = pl.program_id(0)
 
     @pl.when(t == 0)
@@ -63,25 +63,30 @@
         num_ref[...] = jnp.zeros_like(num_ref)
         mass_ref[...] = jnp.zeros_like(mass_ref)
 
-    x = pts_ref[...]
-    ids = [ids_ref[t, s] for s in range(SLOTS)]
-    cands = jnp.concatenate([cand_ref[i] for i in ids], axis=0)
-    offs = jnp.concatenate([off_ref[i] for i in ids], axis=1)
-    scores = lax.dot_general(
-        x, cands, (((1,), (1,)), ((), ())), preferred_element_type=jnp.float32
-    ) * (32.0 / D)
-    scores = scores + offs
-    top = jnp.max(scores, axis=-1, keepdims=True)
-    unnorm = jnp.exp(scores - top)
-    member = (unnorm / jnp.sum(unnorm, axis=-1, keepdims=True)).astype(jnp.bfloat16)
-    mass = jnp.sum(member.astype(jnp.float32), axis=0, keepdims=True)
-    num = lax.dot_general(
-        member, x, (((0,), (0,)), ((), ())), preferred_element_type=jnp.float32
-    )
-    for s in range(SLOTS):
-        i = ids[s]
-        num_ref[i] += num[s * BLOCK:(s + 1) * BLOCK]
-        mass_ref[i] += mass[:, s * BLOCK:(s + 1) * BLOCK]
+    for k in range(per_step):
+        tile = t * per_step + k
+        x = pts_ref[k * TILE:(k + 1) * TILE, :]
+        ids = [ids_ref[tile, s] for s in range(SLOTS)]
+        cands = jnp.concatenate([cand_ref[i] for i in ids], axis=0)
+        offs = jnp.concatenate([off_ref[i] for i in ids], axis=1)
+        scores = lax.dot_general(
+            x, cands, (((1,), (1,)), ((), ())), preferred_element_type=jnp.float32
+        ) * (32.0 / D)
+        scores = scores + offs
+        top = jnp.max(scores, axis=-1, keepdims=True)
+        unnorm = jnp.exp(scores - top)
+        member = (unnorm / jnp.sum(unnorm, axis=-1, keepdims=True)).astype(jnp.bfloat16)
+        mass = jnp.sum(member.astype(jnp.float32), axis=0, keepdims=True)
+        num = lax.dot_general(
+            member, x, (((0,), (0,)), ((), ())), preferred_element_type=jnp.float32
+        )
+        for s in range(SLOTS):
+            i = ids[s]
+            num_ref[i] += num[s * BLOCK:(s + 1) * BLOCK]
+            mass_ref[i] += mass[:, s * BLOCK:(s + 1) * BLOCK]
+
+
+PER_STEP = 8
 
 
 def assign_tiles(points, near_ids, near_centroids, offsets):
@@ -92,16 +97,16 @@
     off = offsets.reshape(block_total, 1, BLOCK)
     flops = 4 * tile_count * TILE * SLOTS * BLOCK * width
     num, mass = pl.pallas_call(
-        tile_kernel,
+        functools.partial(tile_kernel, PER_STEP),
         out_shape=(
             jax.ShapeDtypeStruct((block_total, BLOCK, width), jnp.float32),
             jax.ShapeDtypeStruct((block_total, 1, BLOCK), jnp.float32),
         ),
         grid_spec=pltpu.PrefetchScalarGridSpec(
             num_scalar_prefetch=1,
-            grid=(tile_count,),
+            grid=(tile_count // PER_STEP,),
             in_specs=[
-                pl.BlockSpec((TILE, width), lambda t, ids: (t, 0)),
+                pl.BlockSpec((TILE * PER_STEP, width), lambda t, ids: (t, 0)),
                 pl.BlockSpec((block_total, BLOCK, width), lambda t, ids: (0, 0, 0)),
                 pl.BlockSpec((block_total, 1, BLOCK), lambda t, ids: (0, 0, 0)),
             ],

time: 567 us -> 503 us (0.89)
  Pallas kernels: 133 us -> 71.8 us
    pallas_call x2, Pallas kernels: 133 us -> 71.8 us  [assign_tiles(): pl.pallas_call(functools.partial(tile_kernel, PER_STEP), out_shape=(jax.S...]
where the time goes in v2:
time: 503 us
  waiting for transfers between devices  321 us (64%)
  Pallas kernels  71.8 us (14%)
  starting transfers between devices  38.9 us (8%)
  blocking collectives  20.9 us (4%)
  other arithmetic  18.6 us (4%)
  local copies, waits for them, and re-layouts  17.6 us (3%)
  between operations  14.2 us (3%)
    ppermute x8, waiting for transfers between devices, passed_along(): return lax.ppermute(block, axis, route)  155 us
    psum x2, waiting for transfers between devices, per_device(): total_num, total_mass = lax.psum((own_num, own_mass), 'group')  111 us
    pallas_call x2, Pallas kernels, assign_tiles(): pl.pallas_call(functools.partial(tile_kernel, PER_STEP), out_shape=(jax.S...  71.8 us
    ppermute x4, waiting for transfers between devices, with_halo(): lax.ppermute(tail, axis, [(i, (i + 1) % count) for i in range(count)])  55 us
    ppermute x4, starting transfers between devices, with_halo(): lax.ppermute(head, axis, [((i + 1) % count, i) for i in range(count)])  21.7 us
    psum x2, blocking collectives, per_device(): total_num, total_mass = lax.psum((own_num, own_mass), 'group')  20.9 us
    ppermute x8, starting transfers between devices, passed_along(): return lax.ppermute(block, axis, route)  13.7 us
  transfers between devices with their start and end apart: 18, of which 12 were waited for; matrix products, arithmetic and copies ran while one was open for 1% of the time, Pallas kernels for 0%

profile of v2, /device:TPU:1, one launch (start us, length us, event | category | flops | bytes accessed | tf_op | source)
XLA Modules:
  0.0 502.5 jit_solution(3018962903504371526)
XLA Ops:
  7.2 2.1 collective-permute-start
  9.3 5.8 %collective-permute-start.1 = (bf16[1024,768]{1,0:T(8,128)(2,1)}, bf16[1024,768]{1,0:T(8,128)(2,1)S(1)}, u32[]{:S(2)}, u32[]{:S(2)}) collective-permute-start(bf16[1024,768]{1,0:T(8,128)(2,1)} %param.6), channel_id=1, source_target_pairs={{1,0},{2,1},{3,2},{4,3},{5,4},{6,5},{7,6},{8,7},{9,8},{10,9},{11,1... | collective-permute-start | bytes 4718600 | tf_op jit(solution)/shard_map/ppermute | solution.py:36
  15.2 5.7 %collective-permute-start.3 = (bf16[1024]{0:T(1024)(128)(2,1)}, bf16[1024]{0:T(1024)(128)(2,1)S(1)}, u32[]{:S(2)}, u32[]{:S(2)}) collective-permute-start(bf16[1024]{0:T(1024)(128)(2,1)} %param.7), channel_id=1, source_target_pairs={{1,0},{2,1},{3,2},{4,3},{5,4},{6,5},{7,6},{8,7},{9,8},{10,9},{11,1... | collective-permute-start | bytes 6152 | tf_op jit(solution)/shard_map/ppermute | solution.py:36
  20.9 0.8 copy.10
  21.6 0.7 fusion.6.ids_ref
  22.3 0.8 concatenate.49
  23.0 26.5 %collective-permute-done.2 = bf16[1024]{0:T(1024)(128)(2,1)S(1)} collective-permute-done((bf16[1024]{0:T(1024)(128)(2,1)}, bf16[1024]{0:T(1024)(128)(2,1)S(1)}, u32[]{:S(2)}, u32[]{:S(2)}) %collective-permute-start.2) | collective-permute-done | bytes 2080 | tf_op jit(solution)/shard_map/ppermute | solution.py:34
  49.6 0.1 concatenate.48
  49.6 0.1 concatenate.50
  49.7 1.5 constant_dynamic-update-slice_fusion.2
  51.3 0.1 constant_dynamic-update-slice_fusion.1
  51.4 0.1 constant_dynamic-update-slice_fusion
  51.5 2.2 copy-done
  53.7 1.0 multiply_reduce_fusion.1
  54.7 0.1 mul.38
  54.8 0.7 fusion.8.off_ref
  55.5 35.9 %shard_map.59 = (f32[48,64,768]{2,1,0:T(8,128)}, f32[48,1,64]{2,1,0:T(1,128)}) custom-call(s32[64,4]{1,0:T(8,128)} %fusion.6.ids_ref, bf16[8192,768]{1,0:T(8,128)(2,1)} %pts_ref.3, bf16[48,64,768]{2,1,0:T(8,128)(2,1)} %bitcast.14, f32[48,1,64]{2,1,0:T(1,128)} %fusion.8.off_ref), custom_call_target="tpu_custom_call" | custom-call | flops 6442450944 | bytes 26738688 | tf_op jit(solution)/shard_map/pallas_call | solution.py:99
  91.4 4.8 fusion.11
  96.2 5.3 %collective-permute-start.4 = (f32[1024,768]{1,0:T(8,128)S(1)}, f32[1024,768]{1,0:T(8,128)S(1)}, u32[]{:S(2)}, u32[]{:S(2)}) collective-permute-start(f32[1024,768]{1,0:T(8,128)S(1)} %bitcast.18), channel_id=1, source_target_pairs={{1,0},{2,1},{3,2},{4,3},{5,4},{6,5},{7,6},{8,7},{9,8},{10,9},{11,1... | collective-permute-start | bytes 9437192 | tf_op jit(solution)/shard_map/ppermute | solution.py:24
  101.6 65.8 %collective-permute-done.4 = f32[1024,768]{1,0:T(8,128)S(1)} collective-permute-done((f32[1024,768]{1,0:T(8,128)S(1)}, f32[1024,768]{1,0:T(8,128)S(1)}, u32[]{:S(2)}, u32[]{:S(2)}) %collective-permute-start.4) | collective-permute-done | bytes 3145760 | tf_op jit(solution)/shard_map/ppermute | solution.py:24
  167.4 6.1 %collective-permute-done.5 = f32[1024,768]{1,0:T(8,128)S(1)} collective-permute-done((f32[1024,768]{1,0:T(8,128)S(1)}, f32[1024,768]{1,0:T(8,128)S(1)}, u32[]{:S(2)}, u32[]{:S(2)}) %collective-permute-start.5) | collective-permute-done | bytes 3145760 | tf_op jit(solution)/shard_map/ppermute | solution.py:24
  173.5 2.3 fusion.1
  175.9 0.0 all-reduce.5.cloned.1.call-start
  175.9 0.7 copy-done.2
  176.6 0.1 slice_reduce_fusion.4
  176.6 0.1 squeeze.40
  176.7 0.3 collective-permute-start.6
  177.0 0.1 squeeze.41
  177.1 1.2 collective-permute-start.7
  178.3 0.1 squeeze.39
  178.3 0.9 collective-permute-done.6
  179.2 4.6 collective-permute-done.7
  183.8 10.5 %psum.29 = f32[1024]{0:T(1024)S(1)} all-reduce(f32[1024]{0:T(1024)S(1)} %add_add_fusion.1), channel_id=1, replica_groups=mesh['group'=4,'blk'=32] {'group'}, use_global_device_ids=true, to_apply=%region_2.3 | all-reduce | flops 1024 | bytes 8192 | tf_op jit(solution)/shard_map/psum | solution.py:149
  194.2 56.3 %all-reduce.3.cloned.1.call-done = f32[1024,768]{1,0:T(8,128)} async-done(((f32[1024,768]{1,0:T(8,128)}), f32[1024,768]{1,0:T(8,128)}) %all-reduce.3.cloned.1.call-update) | async-done | bytes 3145744 | tf_op jit(solution)/shard_map/psum | solution.py:149
  250.5 2.3 divide_convert_fusion.1
  252.8 1.3 collective-permute-start.8
  254.1 4.5 collective-permute-start.9
  258.6 5.7 %collective-permute-start.11 = (bf16[1024]{0:T(1024)(128)(2,1)S(1)}, bf16[1024]{0:T(1024)(128)(2,1)S(1)}, u32[]{:S(2)}, u32[]{:S(2)}) collective-permute-start(bf16[1024]{0:T(1024)(128)(2,1)S(1)} %get-tuple-element.26), channel_id=1, source_target_pairs={{1,0},{2,1},{3,2},{4,3},{5,4},{6,5},{7,6},{8,7},{9,8},{10,9},{11,1... | collective-permute-start | bytes 6152 | tf_op jit(solution)/shard_map/ppermute | solution.py:36
  264.2 0.1 concatenate.52
  264.3 28.5 %collective-permute-done.10 = bf16[1024]{0:T(1024)(128)(2,1)S(1)} collective-permute-done((bf16[1024]{0:T(1024)(128)(2,1)S(1)}, bf16[1024]{0:T(1024)(128)(2,1)S(1)}, u32[]{:S(2)}, u32[]{:S(2)}) %collective-permute-start.10) | collective-permute-done | bytes 2080 | tf_op jit(solution)/shard_map/ppermute | solution.py:34
  292.8 0.1 concatenate.51
  292.9 0.1 concatenate.53
  293.0 4.7 multiply_reduce_fusion
  297.7 0.1 mul.41
  297.8 0.7 fusion.9.off_ref
  298.4 35.9 %shard_map.60 = (f32[48,64,768]{2,1,0:T(8,128)}, f32[48,1,64]{2,1,0:T(1,128)}) custom-call(s32[64,4]{1,0:T(8,128)} %fusion.6.ids_ref, bf16[8192,768]{1,0:T(8,128)(2,1)} %pts_ref.3, bf16[48,64,768]{2,1,0:T(8,128)(2,1)} %bitcast.15, f32[48,1,64]{2,1,0:T(1,128)} %fusion.9.off_ref), custom_call_target="tpu_custom_call" | custom-call | flops 6442450944 | bytes 26738688 | tf_op jit(solution)/shard_map/pallas_call | solution.py:99
  334.3 4.8 fusion.10
  339.2 5.5 %collective-permute-start.12 = (f32[1024,768]{1,0:T(8,128)S(1)}, f32[1024,768]{1,0:T(8,128)S(1)}, u32[]{:S(2)}, u32[]{:S(2)}) collective-permute-start(f32[1024,768]{1,0:T(8,128)S(1)} %bitcast.19), channel_id=1, source_target_pairs={{1,0},{2,1},{3,2},{4,3},{5,4},{6,5},{7,6},{8,7},{9,8},{10,9},{11,1... | collective-permute-start | bytes 9437192 | tf_op jit(solution)/shard_map/ppermute | solution.py:24
  344.6 66.0 %collective-permute-done.12 = f32[1024,768]{1,0:T(8,128)S(1)} collective-permute-done((f32[1024,768]{1,0:T(8,128)S(1)}, f32[1024,768]{1,0:T(8,128)S(1)}, u32[]{:S(2)}, u32[]{:S(2)}) %collective-permute-start.12) | collective-permute-done | bytes 3145760 | tf_op jit(solution)/shard_map/ppermute | solution.py:24
  410.6 6.1 %collective-permute-done.13 = f32[1024,768]{1,0:T(8,128)S(1)} collective-permute-done((f32[1024,768]{1,0:T(8,128)S(1)}, f32[1024,768]{1,0:T(8,128)S(1)}, u32[]{:S(2)}, u32[]{:S(2)}) %collective-permute-start.13) | collective-permute-done | bytes 3145760 | tf_op jit(solution)/shard_map/ppermute | solution.py:24
  416.7 2.3 fusion
  419.1 0.7 copy-done.3
  419.8 0.1 slice_reduce_fusion.1
  419.8 0.1 squeeze.46
  419.9 0.3 collective-permute-start.14
  420.2 0.1 squeeze.47
  420.3 1.2 collective-permute-start.15
  421.5 0.1 squeeze.45
  421.5 0.9 collective-permute-done.14
  422.4 4.6 collective-permute-done.15
  427.0 10.4 %psum.31 = f32[1024]{0:T(1024)S(1)} all-reduce(f32[1024]{0:T(1024)S(1)} %add_add_fusion), channel_id=1, replica_groups=mesh['group'=4,'blk'=32] {'group'}, use_global_device_ids=true, to_apply=%region_5.6 | all-reduce | flops 1024 | bytes 8192 | tf_op jit(solution)/shard_map/psum | solution.py:149
  437.4 0.6 add_convert_fusion
  438.0 54.3 %all-reduce.5.cloned.1.call-done = f32[1024,768]{1,0:T(8,128)} async-done(((f32[1024,768]{1,0:T(8,128)}), f32[1024,768]{1,0:T(8,128)}) %all-reduce.5.cloned.1.call-update) | async-done | bytes 3145744 | tf_op jit(solution)/shard_map/psum | solution.py:149
  492.2 3.4 divide_convert_fusion
  (25 shorter events, 0.1 us)
Async XLA Ops:
  7.2 44.1 %copy-start.1 = (bf16[1024,768]{1,0:T(8,128)(2,1)S(1)}, bf16[1024,768]{1,0:T(8,128)(2,1)}, u32[]{:S(2)}) copy-start(bf16[1024,768]{1,0:T(8,128)(2,1)} %param.6) | copy-start | bytes 4718596
  7.2 243.3 %all-reduce.3.cloned.1.call-start = ((), (), s32[]{:S(2)}) async-start(), calls=%async_computation | async-start | bytes 6291456 | tf_op jit(solution)/shard_map/psum | solution.py:149
  7.2 42.5 %collective-permute-start = (bf16[1024,768]{1,0:T(8,128)(2,1)}, bf16[1024,768]{1,0:T(8,128)(2,1)}, u32[]{:S(2)}, u32[]{:S(2)}) collective-permute-start(bf16[1024,768]{1,0:T(8,128)(2,1)} %param.6), channel_id=1, source_target_pairs={{0,1},{1,2},{2,3},{3,4},{4,5},{5,6},{6,7},{7,8},{8,9},{9,10},{10,1... | collective-permute-start | bytes 4718600 | tf_op jit(solution)/shard_map/ppermute | solution.py:34
  9.3 42.0 %collective-permute-start.1 = (bf16[1024,768]{1,0:T(8,128)(2,1)}, bf16[1024,768]{1,0:T(8,128)(2,1)S(1)}, u32[]{:S(2)}, u32[]{:S(2)}) collective-permute-start(bf16[1024,768]{1,0:T(8,128)(2,1)} %param.6), channel_id=1, source_target_pairs={{1,0},{2,1},{3,2},{4,3},{5,4},{6,5},{7,6},{8,7},{9,8},{10,9},{11,1... | collective-permute-start | bytes 4718600 | tf_op jit(solution)/shard_map/ppermute | solution.py:36
  15.2 34.4 %collective-permute-start.2 = (bf16[1024]{0:T(1024)(128)(2,1)}, bf16[1024]{0:T(1024)(128)(2,1)S(1)}, u32[]{:S(2)}, u32[]{:S(2)}) collective-permute-start(bf16[1024]{0:T(1024)(128)(2,1)} %param.7), channel_id=1, source_target_pairs={{0,1},{1,2},{2,3},{3,4},{4,5},{5,6},{6,7},{7,8},{8,9},{9,10},{10,1... | collective-permute-start | bytes 6152 | tf_op jit(solution)/shard_map/ppermute | solution.py:34
  15.2 34.5 %collective-permute-start.3 = (bf16[1024]{0:T(1024)(128)(2,1)}, bf16[1024]{0:T(1024)(128)(2,1)S(1)}, u32[]{:S(2)}, u32[]{:S(2)}) collective-permute-start(bf16[1024]{0:T(1024)(128)(2,1)} %param.7), channel_id=1, source_target_pairs={{1,0},{2,1},{3,2},{4,3},{5,4},{6,5},{7,6},{8,7},{9,8},{10,9},{11,1... | collective-permute-start | bytes 6152 | tf_op jit(solution)/shard_map/ppermute | solution.py:36
  51.5 2.2 copy-start
  96.2 71.2 %collective-permute-start.4 = (f32[1024,768]{1,0:T(8,128)S(1)}, f32[1024,768]{1,0:T(8,128)S(1)}, u32[]{:S(2)}, u32[]{:S(2)}) collective-permute-start(f32[1024,768]{1,0:T(8,128)S(1)} %bitcast.18), channel_id=1, source_target_pairs={{1,0},{2,1},{3,2},{4,3},{5,4},{6,5},{7,6},{8,7},{9,8},{10,9},{11,1... | collective-permute-start | bytes 9437192 | tf_op jit(solution)/shard_map/ppermute | solution.py:24
  101.6 72.0 %collective-permute-start.5 = (f32[1024,768]{1,0:T(8,128)S(1)}, f32[1024,768]{1,0:T(8,128)S(1)}, u32[]{:S(2)}, u32[]{:S(2)}) collective-permute-start(f32[1024,768]{1,0:T(8,128)S(1)} %bitcast.16), channel_id=1, source_target_pairs={{31,0},{0,1},{1,2},{2,3},{3,4},{4,5},{5,6},{6,7},{7,8},{8,9},{9,10... | collective-permute-start | bytes 9437192 | tf_op jit(solution)/shard_map/ppermute | solution.py:24
  175.8 0.7 copy-start.2
  175.8 18.4 %copy-start.4 = (bf16[1024]{0:T(1024)(128)(2,1)S(1)}, bf16[1024]{0:T(1024)(128)(2,1)}, u32[]{:S(2)}) copy-start(bf16[1024]{0:T(1024)(128)(2,1)} %param.7) | copy-start | bytes 6148
  175.9 316.4 %all-reduce.5.cloned.1.call-start = ((), (), s32[]{:S(2)}) async-start(), calls=%async_computation.1 | async-start | bytes 6291456 | tf_op jit(solution)/shard_map/psum | solution.py:149
  176.7 2.5 collective-permute-start.6
  177.1 6.7 %collective-permute-start.7 = (f32[1024]{0:T(1024)S(1)}, f32[1024]{0:T(1024)S(1)}, u32[]{:S(2)}, u32[]{:S(2)}) collective-permute-start(f32[1024]{0:T(1024)S(1)} %squeeze.41), channel_id=1, source_target_pairs={{31,0},{0,1},{1,2},{2,3},{3,4},{4,5},{5,6},{6,7},{7,8},{8,9},{9,10... | collective-permute-start | bytes 12296 | tf_op jit(solution)/shard_map/ppermute | solution.py:24
  252.8 40.2 %collective-permute-start.8 = (bf16[1024,768]{1,0:T(8,128)(2,1)S(1)}, bf16[1024,768]{1,0:T(8,128)(2,1)S(1)}, u32[]{:S(2)}, u32[]{:S(2)}) collective-permute-start(bf16[1024,768]{1,0:T(8,128)(2,1)S(1)} %divide_convert_fusion.1), channel_id=1, source_target_pairs={{0,1},{1,2},{2,3},{3,4},{4,5},{5,6},{6,7},{7,8},{8,9},{9,10},{10,1... | collective-permute-start | bytes 4718600 | tf_op jit(solution)/shard_map/ppermute | solution.py:34
  254.1 38.9 %collective-permute-start.9 = (bf16[1024,768]{1,0:T(8,128)(2,1)S(1)}, bf16[1024,768]{1,0:T(8,128)(2,1)}, u32[]{:S(2)}, u32[]{:S(2)}) collective-permute-start(bf16[1024,768]{1,0:T(8,128)(2,1)S(1)} %divide_convert_fusion.1), channel_id=1, source_target_pairs={{1,0},{2,1},{3,2},{4,3},{5,4},{6,5},{7,6},{8,7},{9,8},{10,9},{11,1... | collective-permute-start | bytes 4718600 | tf_op jit(solution)/shard_map/ppermute | solution.py:36
  258.6 34.3 %collective-permute-start.10 = (bf16[1024]{0:T(1024)(128)(2,1)S(1)}, bf16[1024]{0:T(1024)(128)(2,1)S(1)}, u32[]{:S(2)}, u32[]{:S(2)}) collective-permute-start(bf16[1024]{0:T(1024)(128)(2,1)S(1)} %get-tuple-element.26), channel_id=1, source_target_pairs={{0,1},{1,2},{2,3},{3,4},{4,5},{5,6},{6,7},{7,8},{8,9},{9,10},{10,1... | collective-permute-start | bytes 6152 | tf_op jit(solution)/shard_map/ppermute | solution.py:34
  258.6 34.3 %collective-permute-start.11 = (bf16[1024]{0:T(1024)(128)(2,1)S(1)}, bf16[1024]{0:T(1024)(128)(2,1)S(1)}, u32[]{:S(2)}, u32[]{:S(2)}) collective-permute-start(bf16[1024]{0:T(1024)(128)(2,1)S(1)} %get-tuple-element.26), channel_id=1, source_target_pairs={{1,0},{2,1},{3,2},{4,3},{5,4},{6,5},{7,6},{8,7},{9,8},{10,9},{11,1... | collective-permute-start | bytes 6152 | tf_op jit(solution)/shard_map/ppermute | solution.py:36
  339.2 71.4 %collective-permute-start.12 = (f32[1024,768]{1,0:T(8,128)S(1)}, f32[1024,768]{1,0:T(8,128)S(1)}, u32[]{:S(2)}, u32[]{:S(2)}) collective-permute-start(f32[1024,768]{1,0:T(8,128)S(1)} %bitcast.19), channel_id=1, source_target_pairs={{1,0},{2,1},{3,2},{4,3},{5,4},{6,5},{7,6},{8,7},{9,8},{10,9},{11,1... | collective-permute-start | bytes 9437192 | tf_op jit(solution)/shard_map/ppermute | solution.py:24
  344.6 72.1 %collective-permute-start.13 = (f32[1024,768]{1,0:T(8,128)S(1)}, f32[1024,768]{1,0:T(8,128)S(1)}, u32[]{:S(2)}, u32[]{:S(2)}) collective-permute-start(f32[1024,768]{1,0:T(8,128)S(1)} %bitcast.17), channel_id=1, source_target_pairs={{31,0},{0,1},{1,2},{2,3},{3,4},{4,5},{5,6},{6,7},{7,8},{8,9},{9,10... | collective-permute-start | bytes 9437192 | tf_op jit(solution)/shard_map/ppermute | solution.py:24
  419.0 0.7 copy-start.3
  419.9 2.5 collective-permute-start.14
  420.3 6.7 %collective-permute-start.15 = (f32[1024]{0:T(1024)S(1)}, f32[1024]{0:T(1024)S(1)}, u32[]{:S(2)}, u32[]{:S(2)}) collective-permute-start(f32[1024]{0:T(1024)S(1)} %squeeze.47), channel_id=1, source_target_pairs={{31,0},{0,1},{1,2},{2,3},{3,4},{4,5},{5,6},{6,7},{7,8},{8,9},{9,10... | collective-permute-start | bytes 12296 | tf_op jit(solution)/shard_map/ppermute | solution.py:24
Sparse Core Ops, SparseCore 0:
  176.0 74.4 all-reduce.2
  419.2 73.0 all-reduce.4
